TPU v7x, 32 devices: a whole 2x2x4 slice. The times are simulated.
32 devices in a mesh: sec: 8 (over z, y), tile: 4 (over x, core).
Axes of the slice: x: 2, y: 2, z: 4, core: 2. Of those that a mesh axis runs over, the one named last changes fastest.
Arguments:
- image: bfloat16 [8, 1024, 1024], P('sec', 'tile'), may hold values from -6 to 6
- weight: bfloat16 [8, 1024, 1024], P('sec', 'tile'), may hold values from 0.25 to 4
- lens_filter_taps: float32 [8, 4, 25], P('sec', 'tile'), may hold values from -2 to 2
- block_src: int32 [8, 4, 4, 2], P('sec', 'tile'), may hold values from 0 to 15
- block_dst: int32 [8, 4, 4, 2], P('sec', None, 'tile'), may hold values from 0 to 3, as said below
- valid_count: int32 [8, 4, 4], P('sec', 'tile'), may hold values from 1 to 2, as said below
- anchor: bfloat16 [16, 128, 128], P('tile'), may hold values from -6 to 6
Outputs:
- correlation: float32 [8, 32, 128, 128], P('sec', 'tile')
Inputs may be any that keep to these rules, and one draw needn't show every extreme that they name: `block_dst`: every block of every strip receives at least one live slot. `valid_count`: in every section some strip receives 2 live slots from every tile; block_src and block_dst are 0 in slots at or beyond the valid count.
All inputs are finite; a program needn't handle non-finite values.
Results may differ from a plain program's by a relative error of at most 0.02.
Values may be sent and summed in bfloat16 or wider, within the bound.
A program may use at most 64 MiB of HBM per device.

v0:
```python
import math

import jax
import jax.numpy as jnp
from jax import lax
from jax.sharding import PartitionSpec as P

B = 128
CAP = 2


def extended_2(block, sides, width):
    for axis, dim in sides:
        count = lax.axis_size(axis)
        forward = [(i, i + 1) for i in range(count - 1)]
        backward = [(target, source) for source, target in forward]
        low = lax.ppermute(
            lax.slice_in_dim(block, block.shape[dim] - width, None, axis=dim), axis, forward
        )
        high = lax.ppermute(lax.slice_in_dim(block, 0, width, axis=dim), axis, backward)
        block = jnp.concatenate([low, block, high], axis=dim)
    return block


def from_behind(value, axis, steps):
    count = lax.axis_size(axis)
    first, last = (max(0, -steps), min(count, count - steps))
    return lax.ppermute(value, axis, [(source, source + steps) for source in range(first, last)])


def window_set(strip_blocks, rim_block):
    extended = jnp.concatenate([strip_blocks, rim_block], 0)
    aligned = extended[:-1]
    half_shift = jnp.concatenate([extended[:-1, :, B // 2 :], extended[1:, :, : B // 2]], 2)
    return jnp.stack([aligned, half_shift], 1).reshape(-1, B, B)


def split_table(table):
    high = table.astype(jnp.bfloat16)
    low = (table - high.astype(jnp.float32)).astype(jnp.bfloat16)
    return (high, low)


def right_mult(data, halves):
    first = jnp.einsum("wjk,kl->wjl", data, halves[0], preferred_element_type=jnp.float32)
    return first + jnp.einsum("wjk,kl->wjl", data, halves[1], preferred_element_type=jnp.float32)


def left_mult(halves, data):
    first = jnp.einsum("jk,wkl->wjl", halves[0], data, preferred_element_type=jnp.float32)
    return first + jnp.einsum("jk,wkl->wjl", halves[1], data, preferred_element_type=jnp.float32)


def spectra(windows, tables):
    pair_right, pair_left = (tables[0], tables[1])
    right = right_mult(windows, pair_right).astype(jnp.bfloat16)
    from_cos = left_mult(pair_left, right[:, :, :B])
    from_sin = left_mult(pair_left, right[:, :, B:])
    spec_re = from_cos[:, :B] - from_sin[:, B:]
    spec_im = -(from_cos[:, B:] + from_sin[:, :B])
    return (spec_re, spec_im)


def body(image, weight, lens_filter_taps, block_src, block_dst, valid_count, anchor):
    rows_here = image.shape[1]
    cols_here = image.shape[2]
    strip_count = anchor.shape[0]
    padded = extended_2(image, (("tile", 1),), 2)[0]
    padded = jnp.pad(padded, ((0, 0), (2, 2)))
    kernel_taps = lens_filter_taps[0, 0]
    corrected = jnp.zeros((rows_here, cols_here), jnp.float32)
    for row_off in range(5):
        for col_off in range(5):
            corrected = corrected + kernel_taps[row_off * 5 + col_off] * padded[
                row_off : row_off + rows_here, col_off : col_off + cols_here
            ].astype(jnp.float32)
    weighted = (corrected * weight[0].astype(jnp.float32)).astype(jnp.bfloat16)
    tile_blocks = (
        weighted.reshape(rows_here // B, B, cols_here // B, B)
        .transpose(0, 2, 1, 3)
        .reshape(-1, B, B)
    )
    source_ids = block_src[0, 0]
    is_live = jnp.arange(CAP)[None, :] < valid_count[0, 0][:, None]
    picked = tile_blocks[source_ids]
    outgoing = jnp.where(is_live[:, :, None, None], picked, jnp.zeros_like(picked))
    incoming_blocks = lax.all_to_all(outgoing, "tile", split_axis=0, concat_axis=0, tiled=True)
    dest_ids = block_dst[0, :, 0, :]
    indicator_vector = (dest_ids[..., None] == jnp.arange(strip_count)[None, None, :]).astype(
        jnp.bfloat16
    )
    strip_blocks = jnp.einsum(
        "dbm,dbnh->mnh", indicator_vector, incoming_blocks, preferred_element_type=jnp.float32
    ).astype(jnp.bfloat16)
    own_rim, anchor_border = from_behind((strip_blocks[:1], anchor[:1]), "tile", -1)
    positions = jnp.arange(B, dtype=jnp.int32)
    product = positions[:, None] * positions[None, :] % B
    angle = product.astype(jnp.float32) * (2.0 * math.pi / B)
    cosine = jnp.cos(angle)
    sine_table = jnp.sin(angle)
    tables = (
        split_table(jnp.concatenate([cosine, sine_table], 1)),
        split_table(jnp.concatenate([cosine, sine_table], 0)),
    )
    is_first = lax.axis_index("sec") == 0
    current = spectra(window_set(strip_blocks, own_rim), tables)
    previous_section_blocks, prior_rim = from_behind((strip_blocks, own_rim), "sec", 1)
    previous_section_blocks = jnp.where(is_first, anchor, previous_section_blocks)
    prior_rim = jnp.where(is_first, anchor_border, prior_rim)
    earlier = spectra(window_set(previous_section_blocks, prior_rim), tables)
    cur_re, cur_im = current
    pre_re, pre_im = earlier
    cross_re = cur_re * pre_re + cur_im * pre_im
    cross_im = cur_im * pre_re - cur_re * pre_im
    magnitude = jnp.sqrt(cross_re * cross_re + cross_im * cross_im)
    mean_mag = jnp.mean(magnitude, axis=(1, 2), keepdims=True)
    denominator = magnitude + 0.1 * mean_mag + 1e-06
    whitened = jnp.concatenate([cross_re / denominator, cross_im / denominator], 2).astype(
        jnp.bfloat16
    )
    inverse_right = split_table(
        jnp.concatenate(
            [jnp.concatenate([cosine, sine_table], 1), jnp.concatenate([-sine_table, cosine], 1)], 0
        )
    )
    inverse_left = split_table(jnp.concatenate([cosine, -sine_table], 1))
    rows_both = right_mult(whitened, inverse_right).astype(jnp.bfloat16)
    stacked = jnp.concatenate([rows_both[:, :, :B], rows_both[:, :, B:]], 1)
    result = left_mult(inverse_left, stacked)
    return (result / B)[None]


def solution(mesh):
    in_specs = (
        P("sec", "tile", None),
        P("sec", "tile", None),
        P("sec", "tile", None),
        P("sec", "tile", None, None),
        P("sec", None, "tile", None),
        P("sec", "tile", None),
        P("tile", None, None),
    )
    out_specs = P("sec", "tile", None, None)
    return jax.shard_map(body, mesh=mesh, in_specs=in_specs, out_specs=out_specs, check_vma=False)
```

profile of v0, /device:TPU:9, one launch (start us, length us, event | category | flops | bytes accessed | tf_op | source)
XLA Modules:
  0.0 68.8 jit_solution(1151261300932108880)
XLA Ops:
  0.0 0.8 %fusion.99 = (bf16[1,2,1024]{2,1,0:T(2,128)(2,1)S(1)}, bf16[1,2,1024]{2,1,0:T(2,128)(2,1)S(1)}) fusion(bf16[1,256,1024]{2,1,0:T(8,128)(2,1)} %param.7), kind=kLoop, calls=%fused_computation.149 | loop fusion | bytes 16384 | tf_op jit(solution)/shard_map/slice | solution.py:18
  0.8 3.7 %collective-permute-start = (bf16[1,2,1024]{2,1,0:T(2,128)(2,1)S(1)}, bf16[1,2,1024]{2,1,0:T(2,128)(2,1)S(1)}, u32[]{:S(2)}, u32[]{:S(2)}) collective-permute-start(bf16[1,2,1024]{2,1,0:T(2,128)(2,1)S(1)} %get-tuple-element.12), channel_id=1, source_target_pairs={{0,1},{1,2},{2,3},{4,5},{5,6},{6,7},{8,9},{9,10},{10,11},{12,13},{... | collective-permute-start | bytes 12296 | tf_op jit(solution)/shard_map/ppermute | solution.py:17
  4.5 1.9 %collective-permute-start.1 = (bf16[1,2,1024]{2,1,0:T(2,128)(2,1)S(1)}, bf16[1,2,1024]{2,1,0:T(2,128)(2,1)S(1)}, u32[]{:S(2)}, u32[]{:S(2)}) collective-permute-start(bf16[1,2,1024]{2,1,0:T(2,128)(2,1)S(1)} %get-tuple-element.13), channel_id=1, source_target_pairs={{1,0},{2,1},{3,2},{5,4},{6,5},{7,6},{9,8},{10,9},{11,10},{13,12},{... | collective-permute-start | bytes 12296 | tf_op jit(solution)/shard_map/ppermute | solution.py:20
  6.4 0.8 %slice.337 = bf16[1,128,128]{2,1,0:T(8,128)(2,1)S(1)} slice(bf16[4,128,128]{2,1,0:T(8,128)(2,1)} %param.13), slice={[0:1], [0:128], [0:128]} | slice | bytes 65536 | tf_op jit(solution)/shard_map/slice | solution.py:95
  7.2 1.9 %collective-permute-start.4 = (bf16[1,128,128]{2,0,1:T(2,128)(2,1)S(1)}, bf16[1,128,128]{2,0,1:T(2,128)(2,1)S(1)}, u32[]{:S(2)}, u32[]{:S(2)}) collective-permute-start(bf16[1,128,128]{2,0,1:T(2,128)(2,1)S(1)} %copy.101), channel_id=1, source_target_pairs={{1,0},{2,1},{3,2},{5,4},{6,5},{7,6},{9,8},{10,9},{11,10},{13,12},{... | collective-permute-start | bytes 98312 | tf_op jit(solution)/shard_map/ppermute | solution.py:28
  9.2 2.1 %fusion.100 = (f32[1,1,1]{2,1,0:T(1,128)}, f32[1,1,1]{2,1,0:T(1,128)}, f32[1,1,1]{2,1,0:T(1,128)}, f32[1,1,1]{2,1,0:T(1,128)}, f32[1,1,1]{2,1,0:T(1,128)}, /*ind...) fusion(f32[1,1,25]{2,1,0:T(1,128)} %param.9), kind=kLoop, calls=%fused_computation.150 | loop fusion | bytes 152 | tf_op jit(solution)/shard_map/slice | solution.py:74
  11.3 1.6 %fusion.101 = (f32[1,1,1]{2,1,0:T(1,128)}, f32[1,1,1]{2,1,0:T(1,128)}, f32[1,1,1]{2,1,0:T(1,128)}, f32[1,1,1]{2,1,0:T(1,128)}, f32[1,1,1]{2,1,0:T(1,128)}, /*index=5*/f32[1,1,1]{2,1,0:T(1,128)}) fusion(f32[1,1,25]{2,1,0:T(1,128)} %param.9), kind=kLoop, calls=%fused_computation.151 | loop fusion | bytes 48 | tf_op jit(solution)/shard_map/slice | solution.py:74
  12.8 1.1 %constant_dynamic-update-slice_fusion.1 = bf16[1,258,1024]{2,1,0:T(8,128)(2,1)S(1)} fusion(bf16[1,256,1024]{2,1,0:T(8,128)(2,1)} %param.7), kind=kLoop, calls=%fused_computation.129 | loop fusion | bytes 1048576
  14.7 20.9 %fusion.30 = bf16[32,8,8,128]{3,1,2,0:T(8,128)(2,1)S(1)} fusion(bf16[1,256,1024]{2,1,0:T(8,128)(2,1)S(1)} %copy-done.1, f32[]{:T(128)} %bitcast.33, f32[]{:T(128)} %bitcast.32, bf16[1,258,1024]{2,1,0:T(8,128)(2,1)S(1)} %constant_dynamic-update-slice_fusion, f32[]{:T(128)} %bitcast.30, f32[]{:T(128)} %bitcast.29, f32[]{:T(128)} %bitcast.28, f32[]{:T(128)} %bitcast.27, ...), kind=kLoop, calls=%fused_computation.65 | loop fusion | flops 21757952 | bytes 3158116
  35.9 0.6 gather_fusion
  36.6 1.0 %copy.65 = bf16[4,2,128,128]{3,1,2,0:T(2,128)(2,1)} copy(bf16[4,2,128,128]{3,2,1,0:T(8,128)(2,1)S(1)} %broadcast_select_fusion) | data formatting | bytes 524288 | tf_op jit(solution)/shard_map/jit(_where)/select_n | solution.py:86
  37.6 3.5 %all-to-all-start = ((bf16[4,2,128,128]{3,1,2,0:T(2,128)(2,1)}), bf16[4,2,128,128]{3,1,2,0:T(2,128)(2,1)S(1)}, u32[]{:S(2)}, u32[]{:S(2)}) async-start(bf16[4,2,128,128]{3,1,2,0:T(2,128)(2,1)} %copy.65), calls=%async_computation | async-start | bytes 524288 | tf_op jit(solution)/shard_map/all_to_all | solution.py:87
  41.1 5.7 %all-to-all-done = bf16[4,2,128,128]{3,1,2,0:T(2,128)(2,1)S(1)} async-done(((bf16[4,2,128,128]{3,1,2,0:T(2,128)(2,1)}), bf16[4,2,128,128]{3,1,2,0:T(2,128)(2,1)S(1)}, u32[]{:S(2)}, u32[]{:S(2)}) %all-to-all-start) | async-done | bytes 262176 | tf_op jit(solution)/shard_map/all_to_all | solution.py:87
  46.9 0.4 fusion.9
  47.3 2.5 %collective-permute-start.2 = (bf16[1,128,128]{2,0,1:T(2,128)(2,1)S(1)}, bf16[1,128,128]{2,0,1:T(2,128)(2,1)S(1)}, u32[]{:S(2)}, u32[]{:S(2)}) collective-permute-start(bf16[1,128,128]{2,0,1:T(2,128)(2,1)S(1)} %slice.331), channel_id=1, source_target_pairs={{1,0},{2,1},{3,2},{5,4},{6,5},{7,6},{9,8},{10,9},{11,10},{13,12},{... | collective-permute-start | bytes 98312 | tf_op jit(solution)/shard_map/ppermute | solution.py:28
  50.3 3.1 %collective-permute-start.3 = (bf16[4,128,128]{2,0,1:T(4,128)(2,1)S(1)}, bf16[4,128,128]{2,0,1:T(4,128)(2,1)S(1)}, u32[]{:S(2)}, u32[]{:S(2)}) collective-permute-start(bf16[4,128,128]{2,0,1:T(4,128)(2,1)S(1)} %fusion.9), channel_id=1, source_target_pairs={{0,4},{4,8},{8,12},{12,16},{16,20},{20,24},{24,28},{1,5},{5,9},{9,... | collective-permute-start | bytes 393224 | tf_op jit(solution)/shard_map/ppermute | solution.py:28
  53.4 0.3 fusion.53
  54.6 0.3 fusion.45
  54.9 0.3 fusion.42
  55.3 0.3 fusion.3
  55.6 3.5 %collective-permute-start.5 = (bf16[1,128,128]{2,0,1:T(2,128)(2,1)S(1)}, bf16[1,128,128]{2,0,1:T(2,128)(2,1)S(1)}, u32[]{:S(2)}, u32[]{:S(2)}) collective-permute-start(bf16[1,128,128]{2,0,1:T(2,128)(2,1)S(1)} %collective-permute-done.2), channel_id=1, source_target_pairs={{0,4},{4,8},{8,12},{12,16},{16,20},{20,24},{24,28},{1,5},{5,9},{9,... | collective-permute-start | bytes 98312 | tf_op jit(solution)/shard_map/ppermute | solution.py:28
  59.4 3.1 %collective-permute-done.5 = bf16[1,128,128]{2,0,1:T(2,128)(2,1)S(1)} collective-permute-done((bf16[1,128,128]{2,0,1:T(2,128)(2,1)S(1)}, bf16[1,128,128]{2,0,1:T(2,128)(2,1)S(1)}, u32[]{:S(2)}, u32[]{:S(2)}) %collective-permute-start.5) | collective-permute-done | bytes 32800 | tf_op jit(solution)/shard_map/ppermute | solution.py:28
  62.9 0.3 fusion.51
  64.4 0.3 fusion.36
  64.7 0.3 fusion.1
  65.1 0.3 fusion
  65.4 0.6 fusion.33
  66.3 0.3 fusion.32
  66.7 0.3 fusion.6
  67.1 0.3 fusion.31
  67.5 0.4 fusion.8
  67.9 1.0 %copy.83 = f32[1,8,128,128]{3,2,1,0:T(8,128)} copy(f32[1,8,128,128]{2,3,1,0:T(8,128)S(1)} %fusion.8) | data formatting | bytes 1048576 | tf_op jit(solution)/shard_map/broadcast_in_dim | solution.py:130
  (51 shorter events, 4.6 us)
Async XLA Ops:
  0.0 14.5 %copy-start = (bf16[1,256,1024]{2,1,0:T(8,128)(2,1)S(1)}, bf16[1,256,1024]{2,1,0:T(8,128)(2,1)}, u32[]{:S(2)}) copy-start(bf16[1,256,1024]{2,1,0:T(8,128)(2,1)} %param.7) | copy-start | bytes 1572868
  0.0 14.2 %copy-start.3 = (s32[1,1,4,2]{2,3,1,0:T(2,128)S(1)}, s32[1,1,4,2]{2,3,1,0:T(2,128)}, u32[]{:S(2)}) copy-start(s32[1,1,4,2]{2,3,1,0:T(2,128)} %param.10) | copy-start | bytes 100
  0.0 14.4 %copy-start.5 = (s32[1,1,4]{2,1,0:T(1,128)S(1)}, s32[1,1,4]{2,1,0:T(1,128)}, u32[]{:S(2)}) copy-start(s32[1,1,4]{2,1,0:T(1,128)} %param.12) | copy-start | bytes 52
  0.8 13.7 %collective-permute-start = (bf16[1,2,1024]{2,1,0:T(2,128)(2,1)S(1)}, bf16[1,2,1024]{2,1,0:T(2,128)(2,1)S(1)}, u32[]{:S(2)}, u32[]{:S(2)}) collective-permute-start(bf16[1,2,1024]{2,1,0:T(2,128)(2,1)S(1)} %get-tuple-element.12), channel_id=1, source_target_pairs={{0,1},{1,2},{2,3},{4,5},{5,6},{6,7},{8,9},{9,10},{10,11},{12,13},{... | collective-permute-start | bytes 12296 | tf_op jit(solution)/shard_map/ppermute | solution.py:17
  4.5 10.0 %collective-permute-start.1 = (bf16[1,2,1024]{2,1,0:T(2,128)(2,1)S(1)}, bf16[1,2,1024]{2,1,0:T(2,128)(2,1)S(1)}, u32[]{:S(2)}, u32[]{:S(2)}) collective-permute-start(bf16[1,2,1024]{2,1,0:T(2,128)(2,1)S(1)} %get-tuple-element.13), channel_id=1, source_target_pairs={{1,0},{2,1},{3,2},{5,4},{6,5},{7,6},{9,8},{10,9},{11,10},{13,12},{... | collective-permute-start | bytes 12296 | tf_op jit(solution)/shard_map/ppermute | solution.py:20
  7.2 52.2 %collective-permute-start.4 = (bf16[1,128,128]{2,0,1:T(2,128)(2,1)S(1)}, bf16[1,128,128]{2,0,1:T(2,128)(2,1)S(1)}, u32[]{:S(2)}, u32[]{:S(2)}) collective-permute-start(bf16[1,128,128]{2,0,1:T(2,128)(2,1)S(1)} %copy.101), channel_id=1, source_target_pairs={{1,0},{2,1},{3,2},{5,4},{6,5},{7,6},{9,8},{10,9},{11,10},{13,12},{... | collective-permute-start | bytes 98312 | tf_op jit(solution)/shard_map/ppermute | solution.py:28
  12.8 1.9 %copy-start.1 = (bf16[1,256,1024]{2,1,0:T(8,128)(2,1)S(1)}, bf16[1,256,1024]{2,1,0:T(8,128)(2,1)}, u32[]{:S(2)}) copy-start(bf16[1,256,1024]{2,1,0:T(8,128)(2,1)} %param.8) | copy-start | bytes 1572868
  36.5 10.4 %copy-start.4 = (s32[1,4,1,2]{1,3,2,0:T(2,128)S(1)}, s32[1,4,1,2]{1,3,2,0:T(2,128)}, u32[]{:S(2)}) copy-start(s32[1,4,1,2]{1,3,2,0:T(2,128)} %param.11) | copy-start | bytes 100
  37.6 9.3 %all-to-all-start = ((bf16[4,2,128,128]{3,1,2,0:T(2,128)(2,1)}), bf16[4,2,128,128]{3,1,2,0:T(2,128)(2,1)S(1)}, u32[]{:S(2)}, u32[]{:S(2)}) async-start(bf16[4,2,128,128]{3,1,2,0:T(2,128)(2,1)} %copy.65), calls=%async_computation | async-start | bytes 524288 | tf_op jit(solution)/shard_map/all_to_all | solution.py:87
  47.3 6.1 %collective-permute-start.2 = (bf16[1,128,128]{2,0,1:T(2,128)(2,1)S(1)}, bf16[1,128,128]{2,0,1:T(2,128)(2,1)S(1)}, u32[]{:S(2)}, u32[]{:S(2)}) collective-permute-start(bf16[1,128,128]{2,0,1:T(2,128)(2,1)S(1)} %slice.331), channel_id=1, source_target_pairs={{1,0},{2,1},{3,2},{5,4},{6,5},{7,6},{9,8},{10,9},{11,10},{13,12},{... | collective-permute-start | bytes 98312 | tf_op jit(solution)/shard_map/ppermute | solution.py:28
  50.3 12.4 %collective-permute-start.3 = (bf16[4,128,128]{2,0,1:T(4,128)(2,1)S(1)}, bf16[4,128,128]{2,0,1:T(4,128)(2,1)S(1)}, u32[]{:S(2)}, u32[]{:S(2)}) collective-permute-start(bf16[4,128,128]{2,0,1:T(4,128)(2,1)S(1)} %fusion.9), channel_id=1, source_target_pairs={{0,4},{4,8},{8,12},{12,16},{16,20},{20,24},{24,28},{1,5},{5,9},{9,... | collective-permute-start | bytes 393224 | tf_op jit(solution)/shard_map/ppermute | solution.py:28
  55.6 7.0 %copy-start.2 = (bf16[4,128,128]{2,1,0:T(8,128)(2,1)S(1)}, bf16[4,128,128]{2,1,0:T(8,128)(2,1)}, u32[]{:S(2)}) copy-start(bf16[4,128,128]{2,1,0:T(8,128)(2,1)} %param.13) | copy-start | bytes 393220
  55.6 6.9 %collective-permute-start.5 = (bf16[1,128,128]{2,0,1:T(2,128)(2,1)S(1)}, bf16[1,128,128]{2,0,1:T(2,128)(2,1)S(1)}, u32[]{:S(2)}, u32[]{:S(2)}) collective-permute-start(bf16[1,128,128]{2,0,1:T(2,128)(2,1)S(1)} %collective-permute-done.2), channel_id=1, source_target_pairs={{0,4},{4,8},{8,12},{12,16},{16,20},{20,24},{24,28},{1,5},{5,9},{9,... | collective-permute-start | bytes 98312 | tf_op jit(solution)/shard_map/ppermute | solution.py:28
where the time goes:
time: 69.5 us; the launch traced here: 68.8 us
  other arithmetic  24 us (35%)
  starting transfers between devices  20.1 us (29%)
  local copies, waits for them, and re-layouts  9.89 us (14%)
  waiting for transfers between devices  8.85 us (13%)
  matrix products  5.58 us (8%)
    unnamed x1, other arithmetic  20.9 us
    ppermute x4, starting transfers between devices, from_behind(): lax.ppermute(value, axis, [(source, source + steps) for source in range(f...  11 us
    all_to_all x1, waiting for transfers between devices, body(): lax.all_to_all(outgoing, 'tile', split_axis=0, concat_axis=0, tiled=True)  5.74 us
    ppermute x1, starting transfers between devices, extended_2(): lax.ppermute(lax.slice_in_dim(block, block.shape[dim] - width, None, axis...  3.68 us
    slice x2, local copies, waits for them, and re-layouts, body(): kernel_taps[row_off * 5 + col_off]  3.62 us
    all_to_all x1, starting transfers between devices, body(): lax.all_to_all(outgoing, 'tile', split_axis=0, concat_axis=0, tiled=True)  3.5 us
    ppermute x4, waiting for transfers between devices, from_behind(): lax.ppermute(value, axis, [(source, source + steps) for source in range(f...  3.11 us
    ppermute x1, starting transfers between devices, extended_2(): lax.ppermute(lax.slice_in_dim(block, 0, width, axis=dim), axis, backward)  1.92 us
  transfers between devices with their start and end apart: 7, of which 2 were waited for; matrix products, arithmetic and copies ran while one was open for 47% of the time, Pallas kernels for 0%

commit v1 on v0

v1 whole, which is shorter than its diff:
```python
import functools
import math

import jax
import jax.numpy as jnp
import numpy as np
from jax import lax
from jax.experimental import pallas as pl
from jax.experimental.pallas import tpu as pltpu
from jax.sharding import PartitionSpec as P

MESH = pl.DeviceIdType.MESH
EDGE = 16
LANES = 128


def repeat(count, step):
    if count <= 4:
        for i in range(count):
            step(i)
    else:
        pl.loop(0, count)(step)


def dft_tables(size):
    positions = np.arange(size)
    angle = (positions[:, None] * positions[None, :] % size) * (2.0 * math.pi / size)
    cosine, sine = np.cos(angle), np.sin(angle)
    inverse_right = np.block([[cosine, sine], [-sine, cosine]])
    forward_left = np.block([[cosine, -sine], [-sine, -cosine]])
    return jnp.asarray(np.concatenate([inverse_right, forward_left], 0), jnp.bfloat16)


def lens(rows, taps, first, count):
    left, middle, right = rows
    lane = lax.broadcasted_iota(jnp.int32, middle.shape, 1)
    shifted = []
    for off in range(-2, 3):
        if off == 0:
            shifted.append(middle)
        elif off > 0:
            mixed = jnp.where(lane < off, right, middle)
            shifted.append(pltpu.roll(mixed, LANES - off, 1))
        else:
            mixed = jnp.where(lane >= LANES + off, left, middle)
            shifted.append(pltpu.roll(mixed, -off, 1))
    total = None
    n = middle.shape[0]
    for a in range(5):
        part = taps[5 * a] * shifted[0]
        for b in range(1, 5):
            part = part + taps[5 * a + b] * shifted[b]
        if a != 2:
            part = pltpu.roll(part, (2 - a) % n, 0)
        part = part[first : first + count]
        total = part if total is None else total + part
    return total


def kernel(
    sections,
    tiles,
    image,
    weight,
    anchor,
    tables,
    taps_ref,
    src_ref,
    dst_ref,
    valid_ref,
    out,
    img,
    wgt,
    halo,
    out_mid,
    out_edge,
    in_mid,
    in_edge,
    strip,
    pre,
    spec,
    tab,
    load_sem,
    halo_send,
    halo_recv,
    mid_send,
    mid_recv,
    edge_send,
    edge_recv,
    strip_send,
    strip_recv,
):
    sec = lax.axis_index("sec")
    me = lax.axis_index("tile")
    th, tw = image.shape[1:]
    side = strip.shape[1]
    blocks = strip.shape[0] - 1
    cap = in_mid.shape[1]
    across, down = tw // side, th // side
    padded = across + 2
    mid = side - 2 * EDGE

    barrier = pltpu.get_barrier_semaphore()

    def greet(target):
        pl.semaphore_signal(barrier, inc=1, device_id=target, device_id_type=MESH)

    for k in range(1, tiles):
        greet((sec, lax.rem(me + k, tiles)))
    has_next, has_prev = sec < sections - 1, sec > 0
    not_first, not_last = me > 0, me < tiles - 1

    @pl.when(has_next)
    def _():
        greet((sec + 1, me))

    @pl.when(has_next & not_first)
    def _():
        greet((sec + 1, me - 1))

    @pl.when(has_prev)
    def _():
        greet((sec - 1, me))

    @pl.when(has_prev & not_last)
    def _():
        greet((sec - 1, me + 1))

    loads = []
    for r in range(down):
        low, high = max(0, r * side - EDGE), min(th, (r + 1) * side + EDGE)
        place = low - (r * side - EDGE)
        for c in range(across):
            columns = pl.ds(c * side, side)
            loads.append(
                pltpu.make_async_copy(
                    image.at[0, pl.ds(low, high - low), columns],
                    img.at[r * padded + c + 1, pl.ds(place, high - low)],
                    load_sem.at[len(loads)],
                )
            )
            loads.append(
                pltpu.make_async_copy(
                    weight.at[0, pl.ds(r * side, side), columns],
                    wgt.at[r * across + c],
                    load_sem.at[len(loads)],
                )
            )
    table_load = pltpu.make_async_copy(tables, tab, load_sem.at[len(loads)])
    for load in loads:
        load.start()
    table_load.start()

    anchor_load = pltpu.make_async_copy(anchor, pre.at[pl.ds(0, blocks)], strip_recv.at[1])

    @pl.when(sec == 0)
    def _():
        anchor_load.start()

    zeros = jnp.zeros(img.shape[1:], img.dtype)
    for r in range(down):
        img[r * padded] = zeros
        img[(r + 1) * padded - 1] = zeros

    @pl.when(me == 0)
    def _():
        for c in range(across):
            img[c + 1, :EDGE] = zeros[:EDGE]

    @pl.when(me == tiles - 1)
    def _():
        for c in range(across):
            img[(down - 1) * padded + c + 1, EDGE + side :] = zeros[:EDGE]
        strip[blocks] = jnp.zeros((side, side), strip.dtype)
        pre[blocks] = jnp.zeros((side, side), pre.dtype)

    after, before = has_next.astype(jnp.int32), has_prev.astype(jnp.int32)
    peers = after * (1 + not_first.astype(jnp.int32)) + before * (1 + not_last.astype(jnp.int32))
    pl.semaphore_wait(barrier, tiles - 1 + peers)

    def remote(src, dst, send, recv, target):
        return pltpu.make_async_remote_copy(
            src_ref=src,
            dst_ref=dst,
            send_sem=send,
            recv_sem=recv,
            device_id=target,
            device_id_type=MESH,
        )

    halo_down = remote(
        image.at[0, pl.ds(th - EDGE, EDGE)],
        halo.at[0],
        halo_send.at[0],
        halo_recv.at[0],
        (sec, lax.rem(me + 1, tiles)),
    )
    halo_up = remote(
        image.at[0, pl.ds(0, EDGE)],
        halo.at[1],
        halo_send.at[1],
        halo_recv.at[1],
        (sec, lax.rem(me + tiles - 1, tiles)),
    )
    anchor_rim = remote(
        anchor.at[0],
        pre.at[blocks],
        strip_send.at[2],
        strip_recv.at[2],
        (sec, lax.rem(me + tiles - 1, tiles)),
    )

    @pl.when(not_last)
    def _():
        halo_down.start()

    @pl.when(not_first)
    def _():
        halo_up.start()

    @pl.when((sec == 0) & not_first)
    def _():
        anchor_rim.start()

    for load in loads:
        load.wait()

    taps = [taps_ref[0, 0, k] for k in range(25)]
    chips = tiles // 2

    def owner(k):
        chip = lax.rem(me // 2 + 1 + k // 2, chips)
        return chip * 2 + lax.rem(me + 1 + k, 2)

    def picked(target, slot, first, count):
        source = src_ref[0, 0, target, slot]
        place = source + 2 * lax.div(source, across)
        rows = [
            img[place + k, first : first + count + 2 * EDGE].astype(jnp.float32) for k in range(3)
        ]
        rows = [part[EDGE - 8 : EDGE + count + 8] for part in rows]
        corrected = lens(rows, taps, 8, count)
        factor = wgt[source, first : first + count].astype(jnp.float32)
        live = jnp.clip(valid_ref[0, 0, target] - slot, 0, 1).astype(jnp.float32)
        return (corrected * factor * live).astype(jnp.bfloat16)

    def mid_copy(k):
        target = owner(k)
        return remote(
            out_mid.at[target], in_mid.at[me], mid_send.at[target], mid_recv.at[me], (sec, target)
        )

    def edge_copy(k):
        target = owner(k)
        return remote(
            out_edge.at[target],
            in_edge.at[me],
            edge_send.at[target],
            edge_recv.at[me],
            (sec, target),
        )

    def fill_mid(k, ref, place):
        for slot in range(cap):
            for piece in range(0, mid, 32):
                ref[place, slot, piece : piece + 32] = picked(owner(k), slot, EDGE + piece, 32)

    def fill_edge(k, ref, place):
        for slot in range(cap):
            ref[place, slot, :EDGE] = picked(owner(k), slot, 0, EDGE)
            ref[place, slot, EDGE:] = picked(owner(k), slot, side - EDGE, EDGE)

    def send_mid(k):
        fill_mid(k, out_mid, owner(k))
        mid_copy(k).start()

    pl.loop(0, tiles - 1)(send_mid)

    @pl.when(not_first)
    def _():
        halo_down.wait_recv()
        for c in range(across):
            img[c + 1, :EDGE] = halo[0, :, c * side : (c + 1) * side]

    @pl.when(not_last)
    def _():
        halo_up.wait_recv()
        for c in range(across):
            img[(down - 1) * padded + c + 1, EDGE + side :] = halo[
                1, :, c * side : (c + 1) * side
            ]

    def send_edge(k):
        fill_edge(k, out_edge, owner(k))
        edge_copy(k).start()

    pl.loop(0, tiles - 1)(send_edge)
    fill_mid(tiles - 1, in_mid, me)
    fill_edge(tiles - 1, in_edge, me)

    def summed(ref, start, count):
        totals = [None] * blocks
        for t in range(tiles):
            for slot in range(cap):
                value = ref[t, slot, pl.ds(start, count)].astype(jnp.float32)
                place = dst_ref[0, t, 0, slot]
                for j in range(blocks):
                    term = value * (1 - jnp.minimum(jnp.abs(place - j), 1)).astype(jnp.float32)
                    totals[j] = term if totals[j] is None else totals[j] + term
        return [total.astype(strip.dtype) for total in totals]

    def arrive(copy_of):
        def step(k):
            source = owner(k)
            copy_of(k, source).wait_recv()

        return step

    def mid_from(k, source):
        return remote(
            out_mid.at[source], in_mid.at[source], mid_send.at[source], mid_recv.at[source], (sec, source)
        )

    def edge_from(k, source):
        return remote(
            out_edge.at[source], in_edge.at[source], edge_send.at[source], edge_recv.at[source], (sec, source)
        )

    repeat(tiles - 1, arrive(mid_from))
    for piece in range(0, mid, 32):
        for j, value in enumerate(summed(in_mid, piece, 32)):
            strip[j, EDGE + piece : EDGE + piece + 32] = value
    repeat(tiles - 1, arrive(edge_from))
    for j, value in enumerate(summed(in_edge, 0, 2 * EDGE)):
        strip[j, :EDGE] = value[:EDGE]
        strip[j, side - EDGE :] = value[EDGE:]

    onward = remote(
        strip.at[pl.ds(0, blocks)],
        pre.at[pl.ds(0, blocks)],
        strip_send.at[1],
        strip_recv.at[1],
        (lax.rem(sec + 1, sections), me),
    )
    rim = remote(
        strip.at[0],
        strip.at[blocks],
        strip_send.at[0],
        strip_recv.at[0],
        (sec, lax.rem(me + tiles - 1, tiles)),
    )
    onward_rim = remote(
        strip.at[0],
        pre.at[blocks],
        strip_send.at[3],
        strip_recv.at[2],
        (lax.rem(sec + 1, sections), lax.rem(me + tiles - 1, tiles)),
    )

    @pl.when(not_first)
    def _():
        rim.start()

    @pl.when(has_next & not_first)
    def _():
        onward_rim.start()

    @pl.when(has_next)
    def _():
        onward.start()

    table_load.wait()
    right_table = tab.at[pl.ds(0, 2 * side)]
    left_table = tab.at[pl.ds(2 * side, 2 * side)]

    def spectra(ref, m):
        block, after = ref[m], ref[m + 1]
        lane = lax.broadcasted_iota(jnp.int32, block.shape, 1)
        shifted = jnp.where(
            lane < side // 2, after.astype(jnp.float32), block.astype(jnp.float32)
        ).astype(block.dtype)
        windows = jnp.concatenate([block, shifted], 0)
        right = jnp.dot(
            windows, right_table[:side], preferred_element_type=jnp.float32
        ).astype(jnp.bfloat16)
        stacked = jnp.concatenate(
            [
                jnp.concatenate([right[:side, :side], right[:side, side:]], 0),
                jnp.concatenate([right[side:, :side], right[side:, side:]], 0),
            ],
            1,
        )
        return jnp.dot(left_table[...], stacked, preferred_element_type=jnp.float32)

    def keep(m):
        spec[m] = spectra(strip, m)

    repeat(blocks - 1, keep)

    @pl.when(not_last)
    def _():
        rim.wait_recv()

    keep(blocks - 1)

    @pl.when(has_prev)
    def _():
        onward.wait_recv()

    @pl.when(sec == 0)
    def _():
        anchor_load.wait()

    @pl.when(not_last)
    def _():
        anchor_rim.wait_recv()

    def correlate(m):
        earlier = spectra(pre, m)
        current = spec[m]
        cur_re, cur_im = current[:side], current[side:]
        pre_re, pre_im = earlier[:side], earlier[side:]
        cross_re = cur_re * pre_re + cur_im * pre_im
        cross_im = cur_im * pre_re - cur_re * pre_im
        magnitude = jnp.sqrt(cross_re * cross_re + cross_im * cross_im)
        whitened = []
        for half in range(2):
            cols = slice(half * side, (half + 1) * side)
            mag = magnitude[:, cols]
            mean = jnp.sum(mag) * (1.0 / (side * side))
            scale = (1.0 / side) / (mag + (0.1 * mean + 1e-06))
            whitened.append(
                jnp.concatenate([cross_re[:, cols] * scale, cross_im[:, cols] * scale], 1)
            )
        whitened = jnp.concatenate(whitened, 0).astype(jnp.bfloat16)
        rows = jnp.dot(
            whitened, right_table[...], preferred_element_type=jnp.float32
        ).astype(jnp.bfloat16)
        stacked = jnp.concatenate(
            [
                jnp.concatenate([rows[:side, :side], rows[:side, side:]], 0),
                jnp.concatenate([rows[side:, :side], rows[side:, side:]], 0),
            ],
            1,
        )
        result = jnp.dot(left_table[:side], stacked, preferred_element_type=jnp.float32)
        out[0, 2 * m] = result[:, :side]
        out[0, 2 * m + 1] = result[:, side:]

    repeat(blocks, correlate)

    @pl.when(not_last)
    def _():
        halo_down.wait_send()

    @pl.when(not_first)
    def _():
        halo_up.wait_send()
        rim.wait_send()

    @pl.when((sec == 0) & not_first)
    def _():
        anchor_rim.wait_send()

    @pl.when(has_next)
    def _():
        onward.wait_send()

    @pl.when(has_next & not_first)
    def _():
        onward_rim.wait_send()

    def left_here(k):
        mid_copy(k).wait_send()
        edge_copy(k).wait_send()

    repeat(tiles - 1, left_here)


def solution(mesh):
    sections, tiles = mesh.shape["sec"], mesh.shape["tile"]

    def body(image, weight, lens_filter_taps, block_src, block_dst, valid_count, anchor):
        th, tw = image.shape[1:]
        blocks, side = anchor.shape[:2]
        cap = block_src.shape[-1]
        anywhere = pl.BlockSpec(memory_space=pl.ANY)
        scalars = pl.BlockSpec(memory_space=pltpu.SMEM)
        bf16 = jnp.bfloat16
        dma = pltpu.SemaphoreType.DMA
        mid = side - 2 * EDGE
        across, down = tw // side, th // side
        return pl.pallas_call(
            functools.partial(kernel, sections, tiles),
            out_shape=jax.ShapeDtypeStruct((1, 2 * blocks, side, side), jnp.float32),
            in_specs=[anywhere] * 4 + [scalars] * 4,
            out_specs=pl.BlockSpec(memory_space=pltpu.VMEM),
            scratch_shapes=[
                pltpu.VMEM((down * (across + 2), side + 2 * EDGE, side), bf16),
                pltpu.VMEM((down * across, side, side), bf16),
                pltpu.VMEM((2, EDGE, tw), bf16),
                pltpu.VMEM((tiles, cap, mid, side), bf16),
                pltpu.VMEM((tiles, cap, 2 * EDGE, side), bf16),
                pltpu.VMEM((tiles, cap, mid, side), bf16),
                pltpu.VMEM((tiles, cap, 2 * EDGE, side), bf16),
                pltpu.VMEM((blocks + 1, side, side), bf16),
                pltpu.VMEM((blocks + 1, side, side), bf16),
                pltpu.VMEM((blocks, 2 * side, 2 * side), jnp.float32),
                pltpu.VMEM((4 * side, 2 * side), bf16),
                dma((2 * down * across + 1,)),
                dma((2,)),
                dma((2,)),
                dma((tiles,)),
                dma((tiles,)),
                dma((tiles,)),
                dma((tiles,)),
                dma((4,)),
                dma((3,)),
            ],
            compiler_params=pltpu.CompilerParams(collective_id=0, has_side_effects=True),
        )(
            image,
            weight,
            anchor,
            dft_tables(side),
            lens_filter_taps,
            block_src,
            block_dst,
            valid_count,
        )

    in_specs = (
        P("sec", "tile", None),
        P("sec", "tile", None),
        P("sec", "tile", None),
        P("sec", "tile", None, None),
        P("sec", None, "tile", None),
        P("sec", "tile", None),
        P("tile", None, None),
    )
    out_specs = P("sec", "tile", None, None)
    return jax.shard_map(body, mesh=mesh, in_specs=in_specs, out_specs=out_specs, check_vma=False)
```

time: 69.5 us -> 22.6 us (0.33)
  the two profiles are of different devices: /device:TPU:9 before, /device:TPU:24 now
where the time goes in v1:
time: 22.6 us; the launch traced here: 22.4 us
  Pallas kernels  18.5 us (82%)
  local copies, waits for them, and re-layouts  3.89 us (17%)
    pallas_call x1, Pallas kernels, body(): pl.pallas_call(functools.partial(kernel, sections, tiles), out_shape=jax....  18.5 us
    unnamed x5, local copies, waits for them, and re-layouts  3.89 us

profile of v1, /device:TPU:24, one launch (start us, length us, event | category | flops | bytes accessed | tf_op | source)
XLA Modules:
  0.0 22.4 jit_solution(10828001470667877091)
XLA Ops:
  0.0 0.0 copy-start
  0.0 1.3 %copy.9.src_ref = s32[1,1,4,2]{3,2,1,0:T(4,128)} copy(s32[1,1,4,2]{2,3,1,0:T(2,128)} %param.11) | data formatting | bytes 64 | tf_op args[3]
  1.4 0.0 copy-done
  1.4 0.7 %copy.10.dst_ref = s32[1,4,1,2]{3,2,1,0:T(1,128)} copy(s32[1,4,1,2]{1,3,2,0:T(2,128)S(1)} %copy-done) | data formatting | bytes 64 | tf_op args[4]
  2.0 18.5 %shard_map.82 = f32[1,8,128,128]{3,2,1,0:T(8,128)} custom-call(bf16[1,256,1024]{2,1,0:T(8,128)(2,1)} %image.1, bf16[1,256,1024]{2,1,0:T(8,128)(2,1)} %weight.1, bf16[4,128,128]{2,1,0:T(8,128)(2,1)} %anchor.1, bf16[512,256]{1,0:T(8,128)(2,1)} %constant.2.clone.tables, f32[1,1,25]{2,1,0:T(1,128)} %taps_ref.1, s32[1,1,4,2]{3,2,1,0:T(4,128)} %copy.9.src_ref, ...), custom_call_target="tpu_custom_call" | custom-call | tf_op jit(solution)/shard_map/pallas_call | solution.py:493
  20.5 1.9 %copy.12 = f32[1,8,128,128]{3,2,1,0:T(8,128)} copy(f32[1,8,128,128]{3,2,1,0:T(8,128)} %shard_map.82) | data formatting | bytes 1048576
Async XLA Ops:
  0.0 1.4 %copy-start = (s32[1,4,1,2]{1,3,2,0:T(2,128)S(1)}, s32[1,4,1,2]{1,3,2,0:T(2,128)}, u32[]{:S(2)}) copy-start(s32[1,4,1,2]{1,3,2,0:T(2,128)} %param.12) | copy-start | bytes 100

commit v2 on v1

--- a/solution.py
+++ b/solution.py
@@ -76,8 +76,10 @@
     out_edge,
     in_mid,
     in_edge,
-    strip,
-    pre,
+    strip_mid,
+    strip_edge,
+    pre_mid,
+    pre_edge,
     spec,
     tab,
     load_sem,
@@ -93,8 +95,8 @@
     sec = lax.axis_index("sec")
     me = lax.axis_index("tile")
     th, tw = image.shape[1:]
-    side = strip.shape[1]
-    blocks = strip.shape[0] - 1
+    side = wgt.shape[1]
+    blocks = strip_mid.shape[0] - 1
     cap = in_mid.shape[1]
     across, down = tw // side, th // side
     padded = across + 2
@@ -151,11 +153,22 @@
         load.start()
     table_load.start()
 
-    anchor_load = pltpu.make_async_copy(anchor, pre.at[pl.ds(0, blocks)], strip_recv.at[1])
+    own = pl.ds(0, blocks)
+    inner, upper, lower = pl.ds(EDGE, mid), pl.ds(0, EDGE), pl.ds(side - EDGE, EDGE)
+    anchor_loads = [
+        pltpu.make_async_copy(anchor.at[:, inner], pre_mid.at[own], load_sem.at[len(loads) + 1]),
+        pltpu.make_async_copy(
+            anchor.at[:, upper], pre_edge.at[own, pl.ds(0, EDGE)], load_sem.at[len(loads) + 2]
+        ),
+        pltpu.make_async_copy(
+            anchor.at[:, lower], pre_edge.at[own, pl.ds(EDGE, EDGE)], load_sem.at[len(loads) + 3]
+        ),
+    ]
 
     @pl.when(sec == 0)
     def _():
-        anchor_load.start()
+        for load in anchor_loads:
+            load.start()
 
     zeros = jnp.zeros(img.shape[1:], img.dtype)
     for r in range(down):
@@ -171,12 +184,8 @@
     def _():
         for c in range(across):
             img[(down - 1) * padded + c + 1, EDGE + side :] = zeros[:EDGE]
-        strip[blocks] = jnp.zeros((side, side), strip.dtype)
-        pre[blocks] = jnp.zeros((side, side), pre.dtype)
-
-    after, before = has_next.astype(jnp.int32), has_prev.astype(jnp.int32)
-    peers = after * (1 + not_first.astype(jnp.int32)) + before * (1 + not_last.astype(jnp.int32))
-    pl.semaphore_wait(barrier, tiles - 1 + peers)
+        for ref in (strip_mid, strip_edge, pre_mid, pre_edge):
+            ref[blocks] = jnp.zeros(ref.shape[1:], ref.dtype)
 
     def remote(src, dst, send, recv, target):
         return pltpu.make_async_remote_copy(
@@ -202,25 +211,47 @@
         halo_recv.at[1],
         (sec, lax.rem(me + tiles - 1, tiles)),
     )
-    anchor_rim = remote(
-        anchor.at[0],
-        pre.at[blocks],
-        strip_send.at[2],
-        strip_recv.at[2],
-        (sec, lax.rem(me + tiles - 1, tiles)),
-    )
-
-    @pl.when(not_last)
-    def _():
-        halo_down.start()
-
-    @pl.when(not_first)
-    def _():
-        halo_up.start()
-
-    @pl.when((sec == 0) & not_first)
-    def _():
-        anchor_rim.start()
+    before_me = lax.rem(me + tiles - 1, tiles)
+    next_sec = lax.rem(sec + 1, sections)
+    anchor_rims = [
+        remote(anchor.at[0, rows], ref, strip_send.at[n], strip_recv.at[n], (sec, before_me))
+        for n, (rows, ref) in enumerate(
+            (
+                (inner, pre_mid.at[blocks]),
+                (upper, pre_edge.at[blocks, pl.ds(0, EDGE)]),
+                (lower, pre_edge.at[blocks, pl.ds(EDGE, EDGE)]),
+            )
+        )
+    ]
+
+    def strip_copies(part, strip, pre):
+        first = 3 + 3 * part
+        return [
+            remote(src, dst, strip_send.at[first + n], strip_recv.at[first + n], target)
+            for n, (src, dst, target) in enumerate(
+                (
+                    (strip.at[0], strip.at[blocks], (sec, before_me)),
+                    (strip.at[0], pre.at[blocks], (next_sec, before_me)),
+                    (strip.at[own], pre.at[own], (next_sec, me)),
+                )
+            )
+        ]
+
+    mid_copies = strip_copies(0, strip_mid, pre_mid)
+    edge_copies = strip_copies(1, strip_edge, pre_edge)
+
+    def start_strip(copies):
+        @pl.when(has_next)
+        def _():
+            copies[2].start()
+
+        @pl.when(has_next & not_first)
+        def _():
+            copies[1].start()
+
+        @pl.when(not_first)
+        def _():
+            copies[0].start()
 
     for load in loads:
         load.wait()
@@ -233,7 +264,7 @@
         return chip * 2 + lax.rem(me + 1 + k, 2)
 
     def picked(target, slot, first, count):
-        source = src_ref[0, 0, target, slot]
+        source = src_ref[0, 0, slot, target]
         place = source + 2 * lax.div(source, across)
         rows = [
             img[place + k, first : first + count + 2 * EDGE].astype(jnp.float32) for k in range(3)
@@ -274,7 +305,27 @@
         fill_mid(k, out_mid, owner(k))
         mid_copy(k).start()
 
-    pl.loop(0, tiles - 1)(send_mid)
+    fill_mid(0, out_mid, owner(0))
+    after, before = has_next.astype(jnp.int32), has_prev.astype(jnp.int32)
+    peers = after * (1 + not_first.astype(jnp.int32)) + before * (1 + not_last.astype(jnp.int32))
+    pl.semaphore_wait(barrier, tiles - 1 + peers)
+
+    @pl.when(not_last)
+    def _():
+        halo_down.start()
+
+    @pl.when(not_first)
+    def _():
+        halo_up.start()
+
+    @pl.when((sec == 0) & not_first)
+    def _():
+        for copy in anchor_rims:
+            copy.start()
+
+    mid_copy(0).start()
+    pl.loop(1, tiles - 1)(send_mid)
+    fill_mid(tiles - 1, in_mid, me)
 
     @pl.when(not_first)
     def _():
@@ -295,7 +346,6 @@
         edge_copy(k).start()
 
     pl.loop(0, tiles - 1)(send_edge)
-    fill_mid(tiles - 1, in_mid, me)
     fill_edge(tiles - 1, in_edge, me)
 
     def summed(ref, start, count):
@@ -303,11 +353,11 @@
         for t in range(tiles):
             for slot in range(cap):
                 value = ref[t, slot, pl.ds(start, count)].astype(jnp.float32)
-                place = dst_ref[0, t, 0, slot]
+                place = dst_ref[0, 0, slot, t]
                 for j in range(blocks):
                     term = value * (1 - jnp.minimum(jnp.abs(place - j), 1)).astype(jnp.float32)
                     totals[j] = term if totals[j] is None else totals[j] + term
-        return [total.astype(strip.dtype) for total in totals]
+        return [total.astype(jnp.bfloat16) for total in totals]
 
     def arrive(copy_of):
         def step(k):
@@ -329,52 +379,23 @@
     repeat(tiles - 1, arrive(mid_from))
     for piece in range(0, mid, 32):
         for j, value in enumerate(summed(in_mid, piece, 32)):
-            strip[j, EDGE + piece : EDGE + piece + 32] = value
+            strip_mid[j, piece : piece + 32] = value
+    start_strip(mid_copies)
     repeat(tiles - 1, arrive(edge_from))
     for j, value in enumerate(summed(in_edge, 0, 2 * EDGE)):
-        strip[j, :EDGE] = value[:EDGE]
-        strip[j, side - EDGE :] = value[EDGE:]
-
-    onward = remote(
-        strip.at[pl.ds(0, blocks)],
-        pre.at[pl.ds(0, blocks)],
-        strip_send.at[1],
-        strip_recv.at[1],
-        (lax.rem(sec + 1, sections), me),
-    )
-    rim = remote(
-        strip.at[0],
-        strip.at[blocks],
-        strip_send.at[0],
-        strip_recv.at[0],
-        (sec, lax.rem(me + tiles - 1, tiles)),
-    )
-    onward_rim = remote(
-        strip.at[0],
-        pre.at[blocks],
-        strip_send.at[3],
-        strip_recv.at[2],
-        (lax.rem(sec + 1, sections), lax.rem(me + tiles - 1, tiles)),
-    )
-
-    @pl.when(not_first)
-    def _():
-        rim.start()
-
-    @pl.when(has_next & not_first)
-    def _():
-        onward_rim.start()
-
-    @pl.when(has_next)
-    def _():
-        onward.start()
+        strip_edge[j] = value
+    start_strip(edge_copies)
 
     table_load.wait()
     right_table = tab.at[pl.ds(0, 2 * side)]
     left_table = tab.at[pl.ds(2 * side, 2 * side)]
 
-    def spectra(ref, m):
-        block, after = ref[m], ref[m + 1]
+    def whole(mid_ref, edge_ref, m):
+        edge = edge_ref[m]
+        return jnp.concatenate([edge[:EDGE], mid_ref[m], edge[EDGE:]], 0)
+
+    def spectra(mid_ref, edge_ref, m):
+        block, after = whole(mid_ref, edge_ref, m), whole(mid_ref, edge_ref, m + 1)
         lane = lax.broadcasted_iota(jnp.int32, block.shape, 1)
         shifted = jnp.where(
             lane < side // 2, after.astype(jnp.float32), block.astype(jnp.float32)
@@ -393,30 +414,39 @@
         return jnp.dot(left_table[...], stacked, preferred_element_type=jnp.float32)
 
     def keep(m):
-        spec[m] = spectra(strip, m)
+        spec[m] = spectra(strip_mid, strip_edge, m)
 
     repeat(blocks - 1, keep)
 
     @pl.when(not_last)
     def _():
-        rim.wait_recv()
+        mid_copies[0].wait_recv()
+        edge_copies[0].wait_recv()
 
     keep(blocks - 1)
 
     @pl.when(has_prev)
     def _():
-        onward.wait_recv()
+        mid_copies[2].wait_recv()
+        edge_copies[2].wait_recv()
+
+    @pl.when(has_prev & not_last)
+    def _():
+        mid_copies[1].wait_recv()
+        edge_copies[1].wait_recv()
 
     @pl.when(sec == 0)
     def _():
-        anchor_load.wait()
-
-    @pl.when(not_last)
-    def _():
-        anchor_rim.wait_recv()
+        for load in anchor_loads:
+            load.wait()
+
+    @pl.when((sec == 0) & not_last)
+    def _():
+        for copy in anchor_rims:
+            copy.wait_recv()
 
     def correlate(m):
-        earlier = spectra(pre, m)
+        earlier = spectra(pre_mid, pre_edge, m)
         current = spec[m]
         cur_re, cur_im = current[:side], current[side:]
         pre_re, pre_im = earlier[:side], earlier[side:]
@@ -456,19 +486,23 @@
     @pl.when(not_first)
     def _():
         halo_up.wait_send()
-        rim.wait_send()
+        mid_copies[0].wait_send()
+        edge_copies[0].wait_send()
 
     @pl.when((sec == 0) & not_first)
     def _():
-        anchor_rim.wait_send()
+        for copy in anchor_rims:
+            copy.wait_send()
 
     @pl.when(has_next)
     def _():
-        onward.wait_send()
+        mid_copies[2].wait_send()
+        edge_copies[2].wait_send()
 
     @pl.when(has_next & not_first)
     def _():
-        onward_rim.wait_send()
+        mid_copies[1].wait_send()
+        edge_copies[1].wait_send()
 
     def left_here(k):
         mid_copy(k).wait_send()
@@ -503,19 +537,21 @@
                 pltpu.VMEM((tiles, cap, 2 * EDGE, side), bf16),
                 pltpu.VMEM((tiles, cap, mid, side), bf16),
                 pltpu.VMEM((tiles, cap, 2 * EDGE, side), bf16),
-                pltpu.VMEM((blocks + 1, side, side), bf16),
-                pltpu.VMEM((blocks + 1, side, side), bf16),
+                pltpu.VMEM((blocks + 1, mid, side), bf16),
+                pltpu.VMEM((blocks + 1, 2 * EDGE, side), bf16),
+                pltpu.VMEM((blocks + 1, mid, side), bf16),
+                pltpu.VMEM((blocks + 1, 2 * EDGE, side), bf16),
                 pltpu.VMEM((blocks, 2 * side, 2 * side), jnp.float32),
                 pltpu.VMEM((4 * side, 2 * side), bf16),
-                dma((2 * down * across + 1,)),
+                dma((2 * down * across + 4,)),
                 dma((2,)),
                 dma((2,)),
                 dma((tiles,)),
                 dma((tiles,)),
                 dma((tiles,)),
                 dma((tiles,)),
-                dma((4,)),
-                dma((3,)),
+                dma((9,)),
+                dma((9,)),
             ],
             compiler_params=pltpu.CompilerParams(collective_id=0, has_side_effects=True),
         )(
@@ -524,8 +560,8 @@
             anchor,
             dft_tables(side),
             lens_filter_taps,
-            block_src,
-            block_dst,
+            block_src.transpose(0, 1, 3, 2),
+            block_dst.transpose(0, 2, 3, 1),
             valid_count,
         )
 

time: 22.6 us -> 20.2 us (0.89)
  the two profiles are of different devices: /device:TPU:24 before, /device:TPU:9 now
where the time goes in v2:
time: 20.2 us; the launch traced here: 20 us
  Pallas kernels  18.1 us (90%)
  local copies, waits for them, and re-layouts  1.87 us (9%)
    pallas_call x1, Pallas kernels, body(): pl.pallas_call(functools.partial(kernel, sections, tiles), out_shape=jax....  18.1 us
    unnamed x1, local copies, waits for them, and re-layouts  1.87 us

profile of v2, /device:TPU:9, one launch (start us, length us, event | category | flops | bytes accessed | tf_op | source)
XLA Modules:
  0.0 20.0 jit_solution(12296677384450488526)
XLA Ops:
  0.0 18.1 %shard_map.82 = f32[1,8,128,128]{3,2,1,0:T(8,128)} custom-call(bf16[1,256,1024]{2,1,0:T(8,128)(2,1)} %image.1, bf16[1,256,1024]{2,1,0:T(8,128)(2,1)} %weight.1, bf16[4,128,128]{2,1,0:T(8,128)(2,1)} %anchor.1, bf16[512,256]{1,0:T(8,128)(2,1)} %constant.2.clone.tables, f32[1,1,25]{2,1,0:T(1,128)} %taps_ref.1, s32[1,1,2,4]{3,2,1,0:T(2,128)} %bitcast.2, ...), custom_call_target="tpu_custom_call" | custom-call | tf_op jit(solution)/shard_map/pallas_call | solution.py:527
  18.1 1.9 %copy.10 = f32[1,8,128,128]{3,2,1,0:T(8,128)} copy(f32[1,8,128,128]{3,2,1,0:T(8,128)} %shard_map.82) | data formatting | bytes 1048576

commit v3 on v2

--- a/solution.py
+++ b/solution.py
@@ -64,11 +64,15 @@
     weight,
     anchor,
     tables,
+    taps_any,
+    src_any,
+    dst_any,
+    valid_any,
+    out,
     taps_ref,
     src_ref,
     dst_ref,
     valid_ref,
-    out,
     img,
     wgt,
     halo,
@@ -91,6 +95,7 @@
     edge_recv,
     strip_send,
     strip_recv,
+    anchor_send,
 ):
     sec = lax.axis_index("sec")
     me = lax.axis_index("tile")
@@ -129,6 +134,13 @@
         greet((sec - 1, me + 1))
 
     loads = []
+    for source, ref in (
+        (taps_any, taps_ref),
+        (src_any, src_ref),
+        (dst_any, dst_ref),
+        (valid_any, valid_ref),
+    ):
+        loads.append(pltpu.make_async_copy(source, ref, load_sem.at[len(loads)]))
     for r in range(down):
         low, high = max(0, r * side - EDGE), min(th, (r + 1) * side + EDGE)
         place = low - (r * side - EDGE)
@@ -153,22 +165,20 @@
         load.start()
     table_load.start()
 
-    own = pl.ds(0, blocks)
     inner, upper, lower = pl.ds(EDGE, mid), pl.ds(0, EDGE), pl.ds(side - EDGE, EDGE)
-    anchor_loads = [
-        pltpu.make_async_copy(anchor.at[:, inner], pre_mid.at[own], load_sem.at[len(loads) + 1]),
-        pltpu.make_async_copy(
-            anchor.at[:, upper], pre_edge.at[own, pl.ds(0, EDGE)], load_sem.at[len(loads) + 2]
-        ),
-        pltpu.make_async_copy(
-            anchor.at[:, lower], pre_edge.at[own, pl.ds(EDGE, EDGE)], load_sem.at[len(loads) + 3]
-        ),
-    ]
+    rim_at = 2 * blocks
+
+    def anchor_load(j):
+        for rows, ref, at in (
+            (inner, pre_mid.at[j], 2 * j),
+            (upper, pre_edge.at[j, pl.ds(0, EDGE)], 2 * j + 1),
+            (lower, pre_edge.at[j, pl.ds(EDGE, EDGE)], 2 * j + 1),
+        ):
+            pltpu.make_async_copy(anchor.at[j, rows], ref, strip_recv.at[at]).start()
 
     @pl.when(sec == 0)
     def _():
-        for load in anchor_loads:
-            load.start()
+        repeat(blocks, anchor_load)
 
     zeros = jnp.zeros(img.shape[1:], img.dtype)
     for r in range(down):
@@ -214,44 +224,46 @@
     before_me = lax.rem(me + tiles - 1, tiles)
     next_sec = lax.rem(sec + 1, sections)
     anchor_rims = [
-        remote(anchor.at[0, rows], ref, strip_send.at[n], strip_recv.at[n], (sec, before_me))
-        for n, (rows, ref) in enumerate(
+        remote(anchor.at[0, rows], ref, anchor_send.at[n], strip_recv.at[at], (sec, before_me))
+        for n, (rows, ref, at) in enumerate(
             (
-                (inner, pre_mid.at[blocks]),
-                (upper, pre_edge.at[blocks, pl.ds(0, EDGE)]),
-                (lower, pre_edge.at[blocks, pl.ds(EDGE, EDGE)]),
+                (inner, pre_mid.at[blocks], rim_at),
+                (upper, pre_edge.at[blocks, pl.ds(0, EDGE)], rim_at + 1),
+                (lower, pre_edge.at[blocks, pl.ds(EDGE, EDGE)], rim_at + 1),
             )
         )
     ]
-
-    def strip_copies(part, strip, pre):
-        first = 3 + 3 * part
-        return [
-            remote(src, dst, strip_send.at[first + n], strip_recv.at[first + n], target)
-            for n, (src, dst, target) in enumerate(
-                (
-                    (strip.at[0], strip.at[blocks], (sec, before_me)),
-                    (strip.at[0], pre.at[blocks], (next_sec, before_me)),
-                    (strip.at[own], pre.at[own], (next_sec, me)),
-                )
-            )
-        ]
-
-    mid_copies = strip_copies(0, strip_mid, pre_mid)
-    edge_copies = strip_copies(1, strip_edge, pre_edge)
-
-    def start_strip(copies):
-        @pl.when(has_next)
-        def _():
-            copies[2].start()
-
+    parts = ((strip_mid, pre_mid), (strip_edge, pre_edge))
+
+    def onward(part, j):
+        strip, pre = parts[part]
+        at = 2 * j + part
+        return remote(strip.at[j], pre.at[j], strip_send.at[at], strip_recv.at[at], (next_sec, me))
+
+    def onward_rim(part):
+        strip, pre = parts[part]
+        at = rim_at + part
+        return remote(
+            strip.at[0], pre.at[blocks], strip_send.at[at], strip_recv.at[at], (next_sec, before_me)
+        )
+
+    def own_rim(part):
+        strip, _ = parts[part]
+        at = rim_at + 2 + part
+        return remote(
+            strip.at[0], strip.at[blocks], strip_send.at[at], strip_recv.at[at], (sec, before_me)
+        )
+
+    def start_rims(part):
         @pl.when(has_next & not_first)
         def _():
-            copies[1].start()
+            onward_rim(part).start()
 
         @pl.when(not_first)
         def _():
-            copies[0].start()
+            own_rim(part).start()
+
+    ahead = min(2, blocks)
 
     for load in loads:
         load.wait()
@@ -380,11 +392,30 @@
     for piece in range(0, mid, 32):
         for j, value in enumerate(summed(in_mid, piece, 32)):
             strip_mid[j, piece : piece + 32] = value
-    start_strip(mid_copies)
+    start_rims(0)
+
+    @pl.when(has_next)
+    def _():
+        for j in range(ahead):
+            onward(0, blocks - 1 - j).start()
+
     repeat(tiles - 1, arrive(edge_from))
     for j, value in enumerate(summed(in_edge, 0, 2 * EDGE)):
         strip_edge[j] = value
-    start_strip(edge_copies)
+    start_rims(1)
+
+    @pl.when(has_next)
+    def _():
+        for j in range(ahead):
+            onward(1, blocks - 1 - j).start()
+
+        def later(k):
+            j = blocks - 1 - ahead - k
+            onward(0, j).start()
+            onward(1, j).start()
+
+        repeat(blocks - ahead, later)
+
 
     table_load.wait()
     right_table = tab.at[pl.ds(0, 2 * side)]
@@ -420,32 +451,20 @@
 
     @pl.when(not_last)
     def _():
-        mid_copies[0].wait_recv()
-        edge_copies[0].wait_recv()
+        own_rim(0).wait_recv()
+        own_rim(1).wait_recv()
 
     keep(blocks - 1)
 
-    @pl.when(has_prev)
-    def _():
-        mid_copies[2].wait_recv()
-        edge_copies[2].wait_recv()
-
-    @pl.when(has_prev & not_last)
-    def _():
-        mid_copies[1].wait_recv()
-        edge_copies[1].wait_recv()
-
-    @pl.when(sec == 0)
-    def _():
-        for load in anchor_loads:
-            load.wait()
-
-    @pl.when((sec == 0) & not_last)
-    def _():
-        for copy in anchor_rims:
-            copy.wait_recv()
-
-    def correlate(m):
+    @pl.when(not_last)
+    def _():
+        onward_rim(0).wait_recv()
+        onward_rim(1).wait_recv()
+
+    def correlate(k):
+        m = blocks - 1 - k
+        onward(0, m).wait_recv()
+        onward(1, m).wait_recv()
         earlier = spectra(pre_mid, pre_edge, m)
         current = spec[m]
         cur_re, cur_im = current[:side], current[side:]
@@ -486,8 +505,8 @@
     @pl.when(not_first)
     def _():
         halo_up.wait_send()
-        mid_copies[0].wait_send()
-        edge_copies[0].wait_send()
+        own_rim(0).wait_send()
+        own_rim(1).wait_send()
 
     @pl.when((sec == 0) & not_first)
     def _():
@@ -496,13 +515,16 @@
 
     @pl.when(has_next)
     def _():
-        mid_copies[2].wait_send()
-        edge_copies[2].wait_send()
+        def gone(j):
+            onward(0, j).wait_send()
+            onward(1, j).wait_send()
+
+        repeat(blocks, gone)
 
     @pl.when(has_next & not_first)
     def _():
-        mid_copies[1].wait_send()
-        edge_copies[1].wait_send()
+        onward_rim(0).wait_send()
+        onward_rim(1).wait_send()
 
     def left_here(k):
         mid_copy(k).wait_send()
@@ -519,17 +541,20 @@
         blocks, side = anchor.shape[:2]
         cap = block_src.shape[-1]
         anywhere = pl.BlockSpec(memory_space=pl.ANY)
-        scalars = pl.BlockSpec(memory_space=pltpu.SMEM)
         bf16 = jnp.bfloat16
         dma = pltpu.SemaphoreType.DMA
         mid = side - 2 * EDGE
         across, down = tw // side, th // side
         return pl.pallas_call(
             functools.partial(kernel, sections, tiles),
-            out_shape=jax.ShapeDtypeStruct((1, 2 * blocks, side, side), jnp.float32),
-            in_specs=[anywhere] * 4 + [scalars] * 4,
+            out_shape=pltpu.VMEM((1, 2 * blocks, side, side), jnp.float32),
+            in_specs=[anywhere] * 8,
             out_specs=pl.BlockSpec(memory_space=pltpu.VMEM),
             scratch_shapes=[
+                pltpu.SMEM(lens_filter_taps.shape, jnp.float32),
+                pltpu.SMEM((1, 1, cap, tiles), jnp.int32),
+                pltpu.SMEM((1, 1, cap, tiles), jnp.int32),
+                pltpu.SMEM(valid_count.shape, jnp.int32),
                 pltpu.VMEM((down * (across + 2), side + 2 * EDGE, side), bf16),
                 pltpu.VMEM((down * across, side, side), bf16),
                 pltpu.VMEM((2, EDGE, tw), bf16),
@@ -543,15 +568,16 @@
                 pltpu.VMEM((blocks + 1, 2 * EDGE, side), bf16),
                 pltpu.VMEM((blocks, 2 * side, 2 * side), jnp.float32),
                 pltpu.VMEM((4 * side, 2 * side), bf16),
-                dma((2 * down * across + 4,)),
+                dma((2 * down * across + 5,)),
                 dma((2,)),
                 dma((2,)),
                 dma((tiles,)),
                 dma((tiles,)),
                 dma((tiles,)),
                 dma((tiles,)),
-                dma((9,)),
-                dma((9,)),
+                dma((2 * blocks + 4,)),
+                dma((2 * blocks + 4,)),
+                dma((3,)),
             ],
             compiler_params=pltpu.CompilerParams(collective_id=0, has_side_effects=True),
         )(

time: 20.2 us -> 16.9 us (0.84)
  Pallas kernels: 18.1 us -> 15.9 us
  local copies, waits for them, and re-layouts: 1.87 us -> 0.8 us
    pallas_call x1, Pallas kernels: 18.1 us -> 15.9 us  [body(): pl.pallas_call(functools.partial(kernel, sections, tiles), out_shape=pltp...]
    unnamed x1, local copies, waits for them, and re-layouts: 1.87 us -> 0.8 us
where the time goes in v3:
time: 16.9 us; the launch traced here: 16.7 us
  Pallas kernels  15.9 us (94%)
  local copies, waits for them, and re-layouts  0.8 us (5%)
    pallas_call x1, Pallas kernels, body(): pl.pallas_call(functools.partial(kernel, sections, tiles), out_shape=pltp...  15.9 us
    unnamed x1, local copies, waits for them, and re-layouts  0.8 us

profile of v3, /device:TPU:9, one launch (start us, length us, event | category | flops | bytes accessed | tf_op | source)
XLA Modules:
  0.0 16.7 jit_solution(12829495676090491121)
XLA Ops:
  0.0 15.9 %shard_map.82 = f32[1,8,128,128]{3,2,1,0:T(8,128)S(1)} custom-call(bf16[1,256,1024]{2,1,0:T(8,128)(2,1)} %image.1, bf16[1,256,1024]{2,1,0:T(8,128)(2,1)} %weight.1, bf16[4,128,128]{2,1,0:T(8,128)(2,1)} %anchor.1, bf16[512,256]{1,0:T(8,128)(2,1)} %constant.2.clone.tables, f32[1,1,25]{2,1,0:T(1,128)} %taps_any.1, s32[1,1,2,4]{3,2,1,0:T(2,128)} %bitcast.2, ...), custom_call_target="tpu_custom_call" | custom-call | tf_op jit(solution)/shard_map/pallas_call | solution.py:548
  15.9 0.8 %copy.10 = f32[1,8,128,128]{3,2,1,0:T(8,128)} copy(f32[1,8,128,128]{3,2,1,0:T(8,128)S(1)} %shard_map.82) | data formatting | bytes 1048576

commit v4 on v3

--- a/solution.py
+++ b/solution.py
@@ -76,23 +76,25 @@
     img,
     wgt,
     halo,
-    out_mid,
+    out_a,
+    out_b,
     out_edge,
-    in_mid,
+    in_a,
+    in_b,
     in_edge,
-    strip_mid,
+    strip_a,
+    strip_b,
     strip_edge,
-    pre_mid,
+    pre_a,
+    pre_b,
     pre_edge,
     spec,
     tab,
     load_sem,
     halo_send,
     halo_recv,
-    mid_send,
-    mid_recv,
-    edge_send,
-    edge_recv,
+    block_send,
+    block_recv,
     strip_send,
     strip_recv,
     anchor_send,
@@ -101,11 +103,14 @@
     me = lax.axis_index("tile")
     th, tw = image.shape[1:]
     side = wgt.shape[1]
-    blocks = strip_mid.shape[0] - 1
-    cap = in_mid.shape[1]
+    blocks = strip_a.shape[0] - 1
+    cap = in_a.shape[1]
+    outs, ins = (out_a, out_b, out_edge), (in_a, in_b, in_edge)
+    parts = ((strip_a, pre_a), (strip_b, pre_b), (strip_edge, pre_edge))
+    count = len(parts)
     across, down = tw // side, th // side
     padded = across + 2
-    mid = side - 2 * EDGE
+    mid = strip_a.shape[1]
 
     barrier = pltpu.get_barrier_semaphore()
 
@@ -165,16 +170,21 @@
         load.start()
     table_load.start()
 
-    inner, upper, lower = pl.ds(EDGE, mid), pl.ds(0, EDGE), pl.ds(side - EDGE, EDGE)
-    rim_at = 2 * blocks
+    rim_at = count * blocks
+
+    def anchor_pieces(j):
+        return (
+            (pl.ds(EDGE, mid), pre_a.at[j], 0),
+            (pl.ds(EDGE + mid, mid), pre_b.at[j], 1),
+            (pl.ds(0, EDGE), pre_edge.at[j, pl.ds(0, EDGE)], 2),
+            (pl.ds(side - EDGE, EDGE), pre_edge.at[j, pl.ds(EDGE, EDGE)], 2),
+        )
 
     def anchor_load(j):
-        for rows, ref, at in (
-            (inner, pre_mid.at[j], 2 * j),
-            (upper, pre_edge.at[j, pl.ds(0, EDGE)], 2 * j + 1),
-            (lower, pre_edge.at[j, pl.ds(EDGE, EDGE)], 2 * j + 1),
-        ):
-            pltpu.make_async_copy(anchor.at[j, rows], ref, strip_recv.at[at]).start()
+        for rows, ref, part in anchor_pieces(j):
+            pltpu.make_async_copy(
+                anchor.at[j, rows], ref, strip_recv.at[count * j + part]
+            ).start()
 
     @pl.when(sec == 0)
     def _():
@@ -194,7 +204,7 @@
     def _():
         for c in range(across):
             img[(down - 1) * padded + c + 1, EDGE + side :] = zeros[:EDGE]
-        for ref in (strip_mid, strip_edge, pre_mid, pre_edge):
+        for ref in (strip_a, strip_b, strip_edge, pre_a, pre_b, pre_edge):
             ref[blocks] = jnp.zeros(ref.shape[1:], ref.dtype)
 
     def remote(src, dst, send, recv, target):
@@ -224,20 +234,19 @@
     before_me = lax.rem(me + tiles - 1, tiles)
     next_sec = lax.rem(sec + 1, sections)
     anchor_rims = [
-        remote(anchor.at[0, rows], ref, anchor_send.at[n], strip_recv.at[at], (sec, before_me))
-        for n, (rows, ref, at) in enumerate(
-            (
-                (inner, pre_mid.at[blocks], rim_at),
-                (upper, pre_edge.at[blocks, pl.ds(0, EDGE)], rim_at + 1),
-                (lower, pre_edge.at[blocks, pl.ds(EDGE, EDGE)], rim_at + 1),
-            )
-        )
+        remote(
+            anchor.at[0, rows],
+            ref,
+            anchor_send.at[n],
+            strip_recv.at[rim_at + part],
+            (sec, before_me),
+        )
+        for n, (rows, ref, part) in enumerate(anchor_pieces(blocks))
     ]
-    parts = ((strip_mid, pre_mid), (strip_edge, pre_edge))
 
     def onward(part, j):
         strip, pre = parts[part]
-        at = 2 * j + part
+        at = count * j + part
         return remote(strip.at[j], pre.at[j], strip_send.at[at], strip_recv.at[at], (next_sec, me))
 
     def onward_rim(part):
@@ -249,7 +258,7 @@
 
     def own_rim(part):
         strip, _ = parts[part]
-        at = rim_at + 2 + part
+        at = rim_at + count + part
         return remote(
             strip.at[0], strip.at[blocks], strip_send.at[at], strip_recv.at[at], (sec, before_me)
         )
@@ -263,7 +272,7 @@
         def _():
             own_rim(part).start()
 
-    ahead = min(2, blocks)
+    ahead = min(3, blocks)
 
     for load in loads:
         load.wait()
@@ -287,37 +296,43 @@
         live = jnp.clip(valid_ref[0, 0, target] - slot, 0, 1).astype(jnp.float32)
         return (corrected * factor * live).astype(jnp.bfloat16)
 
-    def mid_copy(k):
+    def block_copy(part, k):
         target = owner(k)
         return remote(
-            out_mid.at[target], in_mid.at[me], mid_send.at[target], mid_recv.at[me], (sec, target)
-        )
-
-    def edge_copy(k):
-        target = owner(k)
+            outs[part].at[target],
+            ins[part].at[me],
+            block_send.at[part, target],
+            block_recv.at[part, me],
+            (sec, target),
+        )
+
+    def block_from(part, k):
+        source = owner(k)
         return remote(
-            out_edge.at[target],
-            in_edge.at[me],
-            edge_send.at[target],
-            edge_recv.at[me],
-            (sec, target),
-        )
-
-    def fill_mid(k, ref, place):
+            outs[part].at[source],
+            ins[part].at[source],
+            block_send.at[part, source],
+            block_recv.at[part, source],
+            (sec, source),
+        )
+
+    def fill(part, k, ref, place):
         for slot in range(cap):
-            for piece in range(0, mid, 32):
-                ref[place, slot, piece : piece + 32] = picked(owner(k), slot, EDGE + piece, 32)
-
-    def fill_edge(k, ref, place):
-        for slot in range(cap):
-            ref[place, slot, :EDGE] = picked(owner(k), slot, 0, EDGE)
-            ref[place, slot, EDGE:] = picked(owner(k), slot, side - EDGE, EDGE)
-
-    def send_mid(k):
-        fill_mid(k, out_mid, owner(k))
-        mid_copy(k).start()
-
-    fill_mid(0, out_mid, owner(0))
+            if part < count - 1:
+                ref[place, slot] = picked(owner(k), slot, EDGE + part * mid, mid)
+            else:
+                ref[place, slot, :EDGE] = picked(owner(k), slot, 0, EDGE)
+                ref[place, slot, EDGE:] = picked(owner(k), slot, side - EDGE, EDGE)
+
+    def send(part, first, last):
+        def step(k):
+            fill(part, k, outs[part], owner(k))
+            block_copy(part, k).start()
+
+        pl.loop(first, last)(step)
+
+    far = tiles - 2
+    fill(0, 0, out_a, owner(0))
     after, before = has_next.astype(jnp.int32), has_prev.astype(jnp.int32)
     peers = after * (1 + not_first.astype(jnp.int32)) + before * (1 + not_last.astype(jnp.int32))
     pl.semaphore_wait(barrier, tiles - 1 + peers)
@@ -335,9 +350,13 @@
         for copy in anchor_rims:
             copy.start()
 
-    mid_copy(0).start()
-    pl.loop(1, tiles - 1)(send_mid)
-    fill_mid(tiles - 1, in_mid, me)
+    block_copy(0, 0).start()
+    send(0, 1, far)
+    send(1, 0, far)
+    send(0, far, tiles - 1)
+    send(1, far, tiles - 1)
+    fill(0, tiles - 1, in_a, me)
+    fill(1, tiles - 1, in_b, me)
 
     @pl.when(not_first)
     def _():
@@ -353,80 +372,49 @@
                 1, :, c * side : (c + 1) * side
             ]
 
-    def send_edge(k):
-        fill_edge(k, out_edge, owner(k))
-        edge_copy(k).start()
-
-    pl.loop(0, tiles - 1)(send_edge)
-    fill_edge(tiles - 1, in_edge, me)
-
-    def summed(ref, start, count):
+    send(2, 0, tiles - 1)
+    fill(2, tiles - 1, in_edge, me)
+
+    def add_up(part):
+        repeat(tiles - 1, lambda k: block_from(part, k).wait_recv())
         totals = [None] * blocks
         for t in range(tiles):
             for slot in range(cap):
-                value = ref[t, slot, pl.ds(start, count)].astype(jnp.float32)
+                value = ins[part][t, slot].astype(jnp.float32)
                 place = dst_ref[0, 0, slot, t]
                 for j in range(blocks):
                     term = value * (1 - jnp.minimum(jnp.abs(place - j), 1)).astype(jnp.float32)
                     totals[j] = term if totals[j] is None else totals[j] + term
-        return [total.astype(jnp.bfloat16) for total in totals]
-
-    def arrive(copy_of):
-        def step(k):
-            source = owner(k)
-            copy_of(k, source).wait_recv()
-
-        return step
-
-    def mid_from(k, source):
-        return remote(
-            out_mid.at[source], in_mid.at[source], mid_send.at[source], mid_recv.at[source], (sec, source)
-        )
-
-    def edge_from(k, source):
-        return remote(
-            out_edge.at[source], in_edge.at[source], edge_send.at[source], edge_recv.at[source], (sec, source)
-        )
-
-    repeat(tiles - 1, arrive(mid_from))
-    for piece in range(0, mid, 32):
-        for j, value in enumerate(summed(in_mid, piece, 32)):
-            strip_mid[j, piece : piece + 32] = value
-    start_rims(0)
+        for j, total in enumerate(totals):
+            parts[part][0][j] = total.astype(jnp.bfloat16)
+        start_rims(part)
+
+        @pl.when(has_next)
+        def _():
+            for k in range(ahead):
+                onward(part, blocks - 1 - k).start()
+
+    for part in range(count):
+        add_up(part)
 
     @pl.when(has_next)
     def _():
-        for j in range(ahead):
-            onward(0, blocks - 1 - j).start()
-
-    repeat(tiles - 1, arrive(edge_from))
-    for j, value in enumerate(summed(in_edge, 0, 2 * EDGE)):
-        strip_edge[j] = value
-    start_rims(1)
-
-    @pl.when(has_next)
-    def _():
-        for j in range(ahead):
-            onward(1, blocks - 1 - j).start()
-
         def later(k):
-            j = blocks - 1 - ahead - k
-            onward(0, j).start()
-            onward(1, j).start()
+            for part in range(count):
+                onward(part, blocks - 1 - ahead - k).start()
 
         repeat(blocks - ahead, later)
-
 
     table_load.wait()
     right_table = tab.at[pl.ds(0, 2 * side)]
     left_table = tab.at[pl.ds(2 * side, 2 * side)]
 
-    def whole(mid_ref, edge_ref, m):
-        edge = edge_ref[m]
-        return jnp.concatenate([edge[:EDGE], mid_ref[m], edge[EDGE:]], 0)
-
-    def spectra(mid_ref, edge_ref, m):
-        block, after = whole(mid_ref, edge_ref, m), whole(mid_ref, edge_ref, m + 1)
+    def whole(which, m):
+        first, second, edge = (pair[which][m] for pair in parts)
+        return jnp.concatenate([edge[:EDGE], first, second, edge[EDGE:]], 0)
+
+    def spectra(which, m):
+        block, after = whole(which, m), whole(which, m + 1)
         lane = lax.broadcasted_iota(jnp.int32, block.shape, 1)
         shifted = jnp.where(
             lane < side // 2, after.astype(jnp.float32), block.astype(jnp.float32)
@@ -445,27 +433,27 @@
         return jnp.dot(left_table[...], stacked, preferred_element_type=jnp.float32)
 
     def keep(m):
-        spec[m] = spectra(strip_mid, strip_edge, m)
+        spec[m] = spectra(0, m)
 
     repeat(blocks - 1, keep)
 
     @pl.when(not_last)
     def _():
-        own_rim(0).wait_recv()
-        own_rim(1).wait_recv()
+        for part in range(count):
+            own_rim(part).wait_recv()
 
     keep(blocks - 1)
 
     @pl.when(not_last)
     def _():
-        onward_rim(0).wait_recv()
-        onward_rim(1).wait_recv()
+        for part in range(count):
+            onward_rim(part).wait_recv()
 
     def correlate(k):
         m = blocks - 1 - k
-        onward(0, m).wait_recv()
-        onward(1, m).wait_recv()
-        earlier = spectra(pre_mid, pre_edge, m)
+        for part in range(count):
+            onward(part, m).wait_recv()
+        earlier = spectra(1, m)
         current = spec[m]
         cur_re, cur_im = current[:side], current[side:]
         pre_re, pre_im = earlier[:side], earlier[side:]
@@ -505,8 +493,8 @@
     @pl.when(not_first)
     def _():
         halo_up.wait_send()
-        own_rim(0).wait_send()
-        own_rim(1).wait_send()
+        for part in range(count):
+            own_rim(part).wait_send()
 
     @pl.when((sec == 0) & not_first)
     def _():
@@ -516,19 +504,19 @@
     @pl.when(has_next)
     def _():
         def gone(j):
-            onward(0, j).wait_send()
-            onward(1, j).wait_send()
+            for part in range(count):
+                onward(part, j).wait_send()
 
         repeat(blocks, gone)
 
     @pl.when(has_next & not_first)
     def _():
-        onward_rim(0).wait_send()
-        onward_rim(1).wait_send()
+        for part in range(count):
+            onward_rim(part).wait_send()
 
     def left_here(k):
-        mid_copy(k).wait_send()
-        edge_copy(k).wait_send()
+        for part in range(count):
+            block_copy(part, k).wait_send()
 
     repeat(tiles - 1, left_here)
 
@@ -543,7 +531,7 @@
         anywhere = pl.BlockSpec(memory_space=pl.ANY)
         bf16 = jnp.bfloat16
         dma = pltpu.SemaphoreType.DMA
-        mid = side - 2 * EDGE
+        mid = (side - 2 * EDGE) // 2
         across, down = tw // side, th // side
         return pl.pallas_call(
             functools.partial(kernel, sections, tiles),
@@ -559,11 +547,15 @@
                 pltpu.VMEM((down * across, side, side), bf16),
                 pltpu.VMEM((2, EDGE, tw), bf16),
                 pltpu.VMEM((tiles, cap, mid, side), bf16),
+                pltpu.VMEM((tiles, cap, mid, side), bf16),
                 pltpu.VMEM((tiles, cap, 2 * EDGE, side), bf16),
+                pltpu.VMEM((tiles, cap, mid, side), bf16),
                 pltpu.VMEM((tiles, cap, mid, side), bf16),
                 pltpu.VMEM((tiles, cap, 2 * EDGE, side), bf16),
                 pltpu.VMEM((blocks + 1, mid, side), bf16),
+                pltpu.VMEM((blocks + 1, mid, side), bf16),
                 pltpu.VMEM((blocks + 1, 2 * EDGE, side), bf16),
+                pltpu.VMEM((blocks + 1, mid, side), bf16),
                 pltpu.VMEM((blocks + 1, mid, side), bf16),
                 pltpu.VMEM((blocks + 1, 2 * EDGE, side), bf16),
                 pltpu.VMEM((blocks, 2 * side, 2 * side), jnp.float32),
@@ -571,13 +563,11 @@
                 dma((2 * down * across + 5,)),
                 dma((2,)),
                 dma((2,)),
-                dma((tiles,)),
-                dma((tiles,)),
-                dma((tiles,)),
-                dma((tiles,)),
-                dma((2 * blocks + 4,)),
-                dma((2 * blocks + 4,)),
-                dma((3,)),
+                dma((3, tiles)),
+                dma((3, tiles)),
+                dma((3 * blocks + 6,)),
+                dma((3 * blocks + 6,)),
+                dma((4,)),
             ],
             compiler_params=pltpu.CompilerParams(collective_id=0, has_side_effects=True),
         )(

time: 16.9 us -> 17 us (level)
  the two profiles are of different devices: /device:TPU:9 before, /device:TPU:1 now
where the time goes in v4:
time: 17 us; the launch traced here: 16.9 us
  Pallas kernels  16 us (94%)
  local copies, waits for them, and re-layouts  0.8 us (5%)
    pallas_call x1, Pallas kernels, body(): pl.pallas_call(functools.partial(kernel, sections, tiles), out_shape=pltp...  16 us
    unnamed x1, local copies, waits for them, and re-layouts  0.8 us

profile of v4, /device:TPU:1, one launch (start us, length us, event | category | flops | bytes accessed | tf_op | source)
XLA Modules:
  0.0 16.9 jit_solution(9985386386354491954)
XLA Ops:
  0.0 16.0 %shard_map.82 = f32[1,8,128,128]{3,2,1,0:T(8,128)S(1)} custom-call(bf16[1,256,1024]{2,1,0:T(8,128)(2,1)} %image.1, bf16[1,256,1024]{2,1,0:T(8,128)(2,1)} %weight.1, bf16[4,128,128]{2,1,0:T(8,128)(2,1)} %anchor.1, bf16[512,256]{1,0:T(8,128)(2,1)} %constant.2.clone.tables, f32[1,1,25]{2,1,0:T(1,128)} %taps_any.1, s32[1,1,2,4]{3,2,1,0:T(2,128)} %bitcast.2, ...), custom_call_target="tpu_custom_call" | custom-call | tf_op jit(solution)/shard_map/pallas_call | solution.py:536
  16.1 0.8 %copy.10 = f32[1,8,128,128]{3,2,1,0:T(8,128)} copy(f32[1,8,128,128]{3,2,1,0:T(8,128)S(1)} %shard_map.82) | data formatting | bytes 1048576

commit v5 on v3

--- a/solution.py
+++ b/solution.py
@@ -263,7 +263,7 @@
         def _():
             own_rim(part).start()
 
-    ahead = min(2, blocks)
+    ahead = 1
 
     for load in loads:
         load.wait()

time: 16.9 us -> 16.8 us (level)
  Pallas kernels: 15.9 us -> 15.7 us
    pallas_call x1, Pallas kernels: 15.9 us -> 15.7 us  [body(): pl.pallas_call(functools.partial(kernel, sections, tiles), out_shape=pltp...]
where the time goes in v5:
time: 16.8 us; the launch traced here: 16.5 us
  Pallas kernels  15.7 us (93%)
  local copies, waits for them, and re-layouts  0.8 us (5%)
    pallas_call x1, Pallas kernels, body(): pl.pallas_call(functools.partial(kernel, sections, tiles), out_shape=pltp...  15.7 us
    unnamed x1, local copies, waits for them, and re-layouts  0.8 us

profile of v5, /device:TPU:9, one launch (start us, length us, event | category | flops | bytes accessed | tf_op | source)
XLA Modules:
  0.0 16.5 jit_solution(11788388359290007282)
XLA Ops:
  0.0 15.7 %shard_map.82 = f32[1,8,128,128]{3,2,1,0:T(8,128)S(1)} custom-call(bf16[1,256,1024]{2,1,0:T(8,128)(2,1)} %image.1, bf16[1,256,1024]{2,1,0:T(8,128)(2,1)} %weight.1, bf16[4,128,128]{2,1,0:T(8,128)(2,1)} %anchor.1, bf16[512,256]{1,0:T(8,128)(2,1)} %constant.2.clone.tables, f32[1,1,25]{2,1,0:T(1,128)} %taps_any.1, s32[1,1,2,4]{3,2,1,0:T(2,128)} %bitcast.2, ...), custom_call_target="tpu_custom_call" | custom-call | tf_op jit(solution)/shard_map/pallas_call | solution.py:548
  15.7 0.8 %copy.10 = f32[1,8,128,128]{3,2,1,0:T(8,128)} copy(f32[1,8,128,128]{3,2,1,0:T(8,128)S(1)} %shard_map.82) | data formatting | bytes 1048576
